TPU v7x, 32 devices: a whole 2x2x4 slice. The times are simulated.
32 devices in a mesh: orb: 4 (over z), tile: 8 (over y, x, core).
Axes of the slice: x: 2, y: 2, z: 4, core: 2. Of those that a mesh axis runs over, the one named last changes fastest.
Arguments:
- basis_values: bfloat16 [2048, 65536], P('tile'), may hold values from -6 to 6
- coefficients: bfloat16 [65536, 128], P('tile', 'orb'), may hold values from -0.03125 to 0.03125
- occupations: float32 [128], P('orb'), may hold values from 0.5 to 2
- owners: int32 [2048, 1], P('tile'), may hold values from 0 to 7; in each aligned block of 256 rows (0 to 255, 256 to 511, ...) at most 64 rows name the same one
- offsets: int32 [2048], P('tile'), may hold values from 0 to 8191
Outputs:
- density: float32 [64, 64, 128], P('tile', 'orb')
- gradient: float32 [3, 64, 64, 128], P(None, 'tile', 'orb')
Inputs may be any that keep to these rules, and one draw needn't show every extreme that they name: `owners`: at most 64 entries of one tile's list name the same owner, and some tile's list reaches 64.
All inputs are finite; a program needn't handle non-finite values.
Results may differ from a plain program's by a relative error of at most 0.0003.
Values may be sent and summed in bfloat16 or wider, within the bound.
A program may use at most 320 MiB of HBM per device.

v0:
```python
import jax
import jax.numpy as jnp
from jax import lax
from jax.sharding import PartitionSpec as P

CY = 64
CZ = 128


def with_halo(cells, sides, width):
    for axis, dim in sides:
        count = lax.axis_size(axis)
        ends = count - 1
        head = lax.slice_in_dim(cells, 0, width, axis=dim)
        tail = lax.slice_in_dim(cells, cells.shape[dim] - width, cells.shape[dim], axis=dim)
        cells = jnp.concatenate(
            [
                lax.ppermute(tail, axis, [(i, (i + 1) % count) for i in range(ends)]),
                cells,
                lax.ppermute(head, axis, [((i + 1) % count, i) for i in range(ends)]),
            ],
            axis=dim,
        )
    return cells


def central(padded):
    along_x = 0.5 * (padded[2:, 1:-1, 1:-1] - padded[:-2, 1:-1, 1:-1])
    along_y = 0.5 * (padded[1:-1, 2:, 1:-1] - padded[1:-1, :-2, 1:-1])
    along_z = 0.5 * (padded[1:-1, 1:-1, 2:] - padded[1:-1, 1:-1, :-2])
    return jnp.stack([along_x, along_y, along_z])


def body(basis_values, coefficients, occupations, owners, offsets):
    listed_count = owners.shape[0]
    rows_held = coefficients.shape[0]
    local_orbitals = coefficients.shape[1]
    owner_ids = owners[:, 0]
    global_rows = owner_ids * rows_held + offsets
    empty = jnp.zeros((listed_count, local_orbitals), jnp.bfloat16)
    shard_rows = lax.all_gather(coefficients, "tile", axis=0, tiled=True)
    inside = (global_rows >= 0) & (global_rows < shard_rows.shape[0])
    safe_rows = jnp.clip(global_rows, 0, shard_rows.shape[0] - 1)
    taken = jnp.take(shard_rows, safe_rows, axis=0)
    listed = jnp.where(inside[:, None], taken, empty)
    depth_cells = basis_values.shape[1] // (CY * CZ)
    share_width = CY // lax.axis_size("orb")
    orbitals = jnp.einsum("bo,bc->oc", listed, basis_values, preferred_element_type=jnp.float32)
    partial_value = jnp.sum(occupations[:, None] * orbitals * orbitals, axis=0).reshape(
        depth_cells, CY, CZ
    )
    density_full = lax.psum(partial_value, "orb")
    padded = with_halo(density_full, (("tile", 0),), 1)
    padded = jnp.pad(padded, ((0, 0), (1, 1), (1, 1)))
    first_col = lax.axis_index("orb") * share_width
    density = lax.dynamic_slice_in_dim(density_full, first_col, share_width, 1)
    gradient = lax.dynamic_slice_in_dim(central(padded), first_col, share_width, 2)
    return (density, gradient)


def solution(mesh):
    placed = (P("tile", None), P("tile", "orb"), P("orb"), P("tile", None), P("tile"))
    return jax.shard_map(
        body,
        mesh=mesh,
        in_specs=placed,
        out_specs=(P("tile", "orb", None), P(None, "tile", "orb", None)),
        check_vma=False,
    )
```

profile of v0, /device:TPU:4, one launch (start us, length us, event | category | flops | bytes accessed | tf_op | source)
XLA Modules:
  0.0 181.8 jit_solution(3366293693858491619)
XLA Ops:
  7.2 0.0 all-gather.2.cloned.1.call-start
  7.2 2.7 %copy.7 = bf16[8192,32]{1,0:T(8,128)(2,1)} copy(bf16[8192,32]{0,1:T(8,128)(2,1)} %param.6) | data formatting | bytes 1048576 | tf_op args[1]
  9.9 0.0 all-gather.2.cloned.1.call-update
  9.9 0.0 all-reduce.3.cloned.1.call-start
  10.0 0.7 broadcast_multiply_fusion
  10.6 0.7 compare_and_fusion
  11.3 88.9 %all-gather.2.cloned.1.call-done = bf16[65536,32]{1,0:T(8,128)(2,1)} async-done(((bf16[8192,32]{1,0:T(8,128)(2,1)}), bf16[65536,32]{1,0:T(8,128)(2,1)}) %all-gather.2.cloned.1.call-update) | async-done | bytes 4194320 | tf_op jit(solution)/shard_map/all_gather | solution.py:41
  100.3 8.7 %gather_fusion = bf16[256,32]{1,0:T(8,128)(2,1)S(1)} fusion(bf16[65536,32]{1,0:T(8,128)(2,1)} %all-gather.2.cloned.1.call-done, s32[1024]{0:T(1024)S(1)} %pad_clamp_fusion), kind=kCustom, calls=%fused_computation | custom fusion | bytes 33792 | tf_op jit(solution)/shard_map/jit(_take)/gather | solution.py:44
  108.9 17.4 %fusion = f32[65536]{0:T(1024)} fusion(f32[32]{0:T(128)} %param.7, bf16[256,65536]{1,0:T(8,128)(2,1)} %param.5, bf16[256,32]{1,0:T(8,128)(2,1)S(1)} %gather_fusion, pred[256]{0:T(512)(128)(4,1)S(1)} %get-tuple-element.2, pred[256]{0:T(512)(128)(4,1)S(1)} %get-tuple-element.8), kind=kOutput, calls=%fused_computation.2 | convolution fusion | flops 1079984128 | bytes 33833600 | tf_op jit(solution)/shard_map/bo,bc->oc/dot_general | solution.py:48
  126.3 0.0 all-reduce.3.cloned.1.call-update
  126.4 36.5 %all-reduce.3.cloned.1.call-done = f32[8,64,128]{2,1,0:T(8,128)} async-done(((f32[8,64,128]{2,1,0:T(8,128)}), f32[8,64,128]{2,1,0:T(8,128)}) %all-reduce.3.cloned.1.call-update) | async-done | bytes 262160 | tf_op jit(solution)/shard_map/psum | solution.py:52
  162.8 0.8 fusion.24
  163.6 1.9 %collective-permute-start = (f32[1,64,128]{2,1,0:T(8,128)S(1)}, f32[1,64,128]{2,1,0:T(8,128)S(1)}, u32[]{:S(2)}, u32[]{:S(2)}) collective-permute-start(f32[1,64,128]{2,1,0:T(8,128)S(1)} %get-tuple-element.6), channel_id=1, source_target_pairs={{1,0},{2,1},{3,2},{4,3},{5,4},{6,5},{7,6},{9,8},{10,9},{11,10},{12... | collective-permute-start | bytes 98312 | tf_op jit(solution)/shard_map/ppermute | solution.py:20
  165.5 2.4 %collective-permute-start.1 = (f32[1,64,128]{2,1,0:T(8,128)S(1)}, f32[1,64,128]{2,1,0:T(8,128)S(1)}, u32[]{:S(2)}, u32[]{:S(2)}) collective-permute-start(f32[1,64,128]{2,1,0:T(8,128)S(1)} %get-tuple-element.7), channel_id=1, source_target_pairs={{0,1},{1,2},{2,3},{3,4},{4,5},{5,6},{6,7},{8,9},{9,10},{10,11},{11... | collective-permute-start | bytes 98312 | tf_op jit(solution)/shard_map/ppermute | solution.py:18
  167.9 1.5 constant_dynamic-slice_fusion
  169.4 0.0 collective-permute-done
  169.4 2.2 %collective-permute-done.1 = f32[1,64,128]{2,1,0:T(8,128)S(1)} collective-permute-done((f32[1,64,128]{2,1,0:T(8,128)S(1)}, f32[1,64,128]{2,1,0:T(8,128)S(1)}, u32[]{:S(2)}, u32[]{:S(2)}) %collective-permute-start.1) | collective-permute-done | bytes 32800 | tf_op jit(solution)/shard_map/ppermute | solution.py:18
  171.7 1.2 select_maximum_fusion
  172.9 1.3 fusion.5
  174.2 0.7 fusion.12
  (1 shorter events, 0.0 us)
Async XLA Ops:
  7.2 93.1 %all-gather.2.cloned.1.call-start = ((), (), s32[]{:S(2)}) async-start(), calls=%async_computation | async-start | bytes 18874368 | tf_op jit(solution)/shard_map/all_gather | solution.py:41
  9.9 152.9 %all-reduce.3.cloned.1.call-start = ((), (), s32[]{:S(2)}) async-start(), calls=%async_computation.1 | async-start | bytes 524288 | tf_op jit(solution)/shard_map/psum | solution.py:52
  163.6 5.8 %collective-permute-start = (f32[1,64,128]{2,1,0:T(8,128)S(1)}, f32[1,64,128]{2,1,0:T(8,128)S(1)}, u32[]{:S(2)}, u32[]{:S(2)}) collective-permute-start(f32[1,64,128]{2,1,0:T(8,128)S(1)} %get-tuple-element.6), channel_id=1, source_target_pairs={{1,0},{2,1},{3,2},{4,3},{5,4},{6,5},{7,6},{9,8},{10,9},{11,10},{12... | collective-permute-start | bytes 98312 | tf_op jit(solution)/shard_map/ppermute | solution.py:20
  165.5 6.1 %collective-permute-start.1 = (f32[1,64,128]{2,1,0:T(8,128)S(1)}, f32[1,64,128]{2,1,0:T(8,128)S(1)}, u32[]{:S(2)}, u32[]{:S(2)}) collective-permute-start(f32[1,64,128]{2,1,0:T(8,128)S(1)} %get-tuple-element.7), channel_id=1, source_target_pairs={{0,1},{1,2},{2,3},{3,4},{4,5},{5,6},{6,7},{8,9},{9,10},{10,11},{11... | collective-permute-start | bytes 98312 | tf_op jit(solution)/shard_map/ppermute | solution.py:18
Sparse Core Ops, SparseCore 0:
  10.0 90.1 all-gather.1
  126.5 36.3 all-reduce.2
where the time goes:
time: 182 us
  waiting for transfers between devices  128 us (70%)
  matrix products  17.4 us (10%)
  between operations  14.1 us (8%)
  local copies, waits for them, and re-layouts  13.6 us (7%)
  other arithmetic  4.62 us (3%)
  starting transfers between devices  4.39 us (2%)
    all_gather x1, waiting for transfers between devices, body(): shard_rows = lax.all_gather(coefficients, 'tile', axis=0, tiled=True)  88.9 us
    psum x1, waiting for transfers between devices, body(): density_full = lax.psum(partial_value, 'orb')  36.5 us
    dot_general x1, matrix products, body(): jnp.einsum('bo,bc->oc', listed, basis_values, preferred_element_type=jnp....  17.4 us
    gather x1, local copies, waits for them, and re-layouts, body(): taken = jnp.take(shard_rows, safe_rows, axis=0)  8.65 us
  transfers between devices with their start and end apart: 4, of which 3 were waited for; matrix products, arithmetic and copies ran while one was open for 2% of the time, Pallas kernels for 0%

commit v1 on v0

--- a/solution.py
+++ b/solution.py
@@ -38,7 +38,20 @@
     owner_ids = owners[:, 0]
     global_rows = owner_ids * rows_held + offsets
     empty = jnp.zeros((listed_count, local_orbitals), jnp.bfloat16)
-    shard_rows = lax.all_gather(coefficients, "tile", axis=0, tiled=True)
+
+    def _watch_scales(v0, ax_name="tile"):
+        many = lax.psum(1, ax_name)
+        r2 = sorted(((c, (c + 1) % many) for c in range(many)))
+        near = v0
+        store = [near]
+        for dev in range(1, many):
+            near = lax.ppermute(near, ax_name, r2)
+            store.insert(0, near)
+        q_next = jnp.concatenate(store, 0)
+        r1 = lax.axis_index(ax_name) + 1
+        return jnp.roll(q_next, r1 * v0.shape[0], axis=0)
+
+    shard_rows = _watch_scales(coefficients)
     inside = (global_rows >= 0) & (global_rows < shard_rows.shape[0])
     safe_rows = jnp.clip(global_rows, 0, shard_rows.shape[0] - 1)
     taken = jnp.take(shard_rows, safe_rows, axis=0)

time: 182 us -> 176 us (0.967)
  waiting for transfers between devices: 128 us -> 104 us
  local copies, waits for them, and re-layouts: 13.6 us -> 30.5 us
    all_gather x1 -> x0, waiting for transfers between devices: 88.9 us -> none  [body(): shard_rows = lax.all_gather(coefficients, 'tile', axis=0, tiled=True)]
    ppermute x0 -> x7, waiting for transfers between devices: none -> 65.6 us  [_watch_scales(): near = lax.ppermute(near, ax_name, r2)]
    unnamed x1 -> x20, local copies, waits for them, and re-layouts: 2.68 us -> 17.3 us
    dynamic_slice x0 -> x1, local copies, waits for them, and re-layouts: none -> 2.23 us  [_watch_scales(): return jnp.roll(q_next, r1 * v0.shape[0], axis=0)]
  transfers between devices with their start and end apart: 4 -> 10, of which waited for: 3 -> 9; matrix products, arithmetic and copies ran while one was open for 2% -> 2% of each run, Pallas kernels for 0% -> 0%
where the time goes in v1:
time: 176 us; the launch traced here: 175 us
  waiting for transfers between devices  104 us (59%)
  local copies, waits for them, and re-layouts  30.5 us (17%)
  matrix products  17.4 us (10%)
  between operations  14.2 us (8%)
  other arithmetic  4.62 us (3%)
  starting transfers between devices  4.43 us (3%)
    ppermute x7, waiting for transfers between devices, _watch_scales(): near = lax.ppermute(near, ax_name, r2)  65.6 us
    psum x1, waiting for transfers between devices, body(): density_full = lax.psum(partial_value, 'orb')  36 us
    dot_general x1, matrix products, body(): jnp.einsum('bo,bc->oc', listed, basis_values, preferred_element_type=jnp....  17.4 us
    unnamed x20, local copies, waits for them, and re-layouts  17.3 us
    gather x1, local copies, waits for them, and re-layouts, body(): taken = jnp.take(shard_rows, safe_rows, axis=0)  8.65 us
  transfers between devices with their start and end apart: 10, of which 9 were waited for; matrix products, arithmetic and copies ran while one was open for 2% of the time, Pallas kernels for 0%

profile of v1, /device:TPU:4, one launch (start us, length us, event | category | flops | bytes accessed | tf_op | source)
XLA Modules:
  0.0 175.0 jit_solution(17970166220957680762)
XLA Ops:
  7.2 0.0 copy-start
  7.2 0.0 all-reduce.3.cloned.1.call-start
  7.2 0.1 collective-permute-start
  7.3 9.7 %collective-permute-done = bf16[8192,32]{0,1:T(8,128)(2,1)S(1)} collective-permute-done((bf16[8192,32]{0,1:T(8,128)(2,1)}, bf16[8192,32]{0,1:T(8,128)(2,1)S(1)}, u32[]{:S(2)}, u32[]{:S(2)}) %collective-permute-start) | collective-permute-done | bytes 524320 | tf_op jit(solution)/shard_map/ppermute | solution.py:48
  17.0 0.0 collective-permute-start.1
  17.0 9.5 %collective-permute-done.1 = bf16[8192,32]{0,1:T(8,128)(2,1)S(1)} collective-permute-done((bf16[8192,32]{0,1:T(8,128)(2,1)S(1)}, bf16[8192,32]{0,1:T(8,128)(2,1)S(1)}, u32[]{:S(2)}, u32[]{:S(2)}) %collective-permute-start.1) | collective-permute-done | bytes 524320 | tf_op jit(solution)/shard_map/ppermute | solution.py:48
  26.5 0.0 collective-permute-start.2
  26.5 9.5 %collective-permute-done.2 = bf16[8192,32]{0,1:T(8,128)(2,1)S(1)} collective-permute-done((bf16[8192,32]{0,1:T(8,128)(2,1)S(1)}, bf16[8192,32]{0,1:T(8,128)(2,1)S(1)}, u32[]{:S(2)}, u32[]{:S(2)}) %collective-permute-start.2) | collective-permute-done | bytes 524320 | tf_op jit(solution)/shard_map/ppermute | solution.py:48
  36.0 0.0 collective-permute-start.3
  36.0 9.5 %collective-permute-done.3 = bf16[8192,32]{0,1:T(8,128)(2,1)S(1)} collective-permute-done((bf16[8192,32]{0,1:T(8,128)(2,1)S(1)}, bf16[8192,32]{0,1:T(8,128)(2,1)S(1)}, u32[]{:S(2)}, u32[]{:S(2)}) %collective-permute-start.3) | collective-permute-done | bytes 524320 | tf_op jit(solution)/shard_map/ppermute | solution.py:48
  45.5 0.0 collective-permute-start.4
  45.5 9.5 %collective-permute-done.4 = bf16[8192,32]{0,1:T(8,128)(2,1)S(1)} collective-permute-done((bf16[8192,32]{0,1:T(8,128)(2,1)S(1)}, bf16[8192,32]{0,1:T(8,128)(2,1)S(1)}, u32[]{:S(2)}, u32[]{:S(2)}) %collective-permute-start.4) | collective-permute-done | bytes 524320 | tf_op jit(solution)/shard_map/ppermute | solution.py:48
  55.0 0.0 collective-permute-start.5
  55.0 9.6 %collective-permute-done.5 = bf16[8192,32]{0,1:T(8,128)(2,1)} collective-permute-done((bf16[8192,32]{0,1:T(8,128)(2,1)S(1)}, bf16[8192,32]{0,1:T(8,128)(2,1)}, u32[]{:S(2)}, u32[]{:S(2)}) %collective-permute-start.5) | collective-permute-done | bytes 524320 | tf_op jit(solution)/shard_map/ppermute | solution.py:48
  64.6 0.0 collective-permute-start.6
  64.6 0.7 broadcast_multiply_fusion
  65.3 0.7 compare_and_fusion
  66.0 8.3 %collective-permute-done.6 = bf16[8192,32]{0,1:T(8,128)(2,1)S(1)} collective-permute-done((bf16[8192,32]{0,1:T(8,128)(2,1)}, bf16[8192,32]{0,1:T(8,128)(2,1)S(1)}, u32[]{:S(2)}, u32[]{:S(2)}) %collective-permute-start.6) | collective-permute-done | bytes 524320 | tf_op jit(solution)/shard_map/ppermute | solution.py:48
  74.4 1.1 constant_dynamic-update-slice_fusion.14
  75.7 1.1 constant_dynamic-update-slice_fusion.8
  76.8 1.1 constant_dynamic-update-slice_fusion.6
  78.1 0.0 copy-done
  78.2 2.2 %constant_dynamic-slice_fusion.1 = bf16[65536,32]{0,1:T(8,128)(2,1)} fusion(bf16[131072,32]{0,1:T(8,128)(2,1)S(1)} %constant_dynamic-update-slice_fusion, s32[]{:T(128)S(6)} %select_n.32), kind=kLoop, calls=%fused_computation.56 | loop fusion | bytes 8388612 | tf_op jit(solution)/shard_map/jit(_roll_dynamic)/dynamic_slice | solution.py:52
  80.4 0.0 copy-start.1
  80.4 13.6 %copy.11 = bf16[65536,32]{1,0:T(8,128)(2,1)} copy(bf16[65536,32]{0,1:T(8,128)(2,1)} %constant_dynamic-slice_fusion.1) | data formatting | bytes 8388608
  94.0 8.7 %gather_fusion = bf16[256,32]{1,0:T(8,128)(2,1)S(1)} fusion(bf16[65536,32]{1,0:T(8,128)(2,1)} %copy.11, s32[1024]{0:T(1024)S(1)} %pad_clamp_fusion), kind=kCustom, calls=%fused_computation | custom fusion | bytes 33792 | tf_op jit(solution)/shard_map/jit(_take)/gather | solution.py:57
  102.6 0.0 copy-done.1
  102.6 17.4 %fusion = f32[65536]{0:T(1024)} fusion(f32[32]{0:T(128)S(1)} %copy-done.1, bf16[256,65536]{1,0:T(8,128)(2,1)} %param.5, bf16[256,32]{1,0:T(8,128)(2,1)S(1)} %gather_fusion, pred[256]{0:T(512)(128)(4,1)S(1)} %get-tuple-element.2, pred[256]{0:T(512)(128)(4,1)S(1)} %get-tuple-element.8), kind=kOutput, calls=%fused_computation.2 | convolution fusion | flops 1079984128 | bytes 33833600 | tf_op jit(solution)/shard_map/bo,bc->oc/dot_general | solution.py:61
  120.1 0.0 all-reduce.3.cloned.1.call-update
  120.1 36.0 %all-reduce.3.cloned.1.call-done = f32[8,64,128]{2,1,0:T(8,128)} async-done(((f32[8,64,128]{2,1,0:T(8,128)}), f32[8,64,128]{2,1,0:T(8,128)}) %all-reduce.3.cloned.1.call-update) | async-done | bytes 262160 | tf_op jit(solution)/shard_map/psum | solution.py:65
  156.1 0.8 fusion.24
  156.9 1.9 %collective-permute-start.7 = (f32[1,64,128]{2,1,0:T(8,128)S(1)}, f32[1,64,128]{2,1,0:T(8,128)S(1)}, u32[]{:S(2)}, u32[]{:S(2)}) collective-permute-start(f32[1,64,128]{2,1,0:T(8,128)S(1)} %get-tuple-element.6), channel_id=1, source_target_pairs={{1,0},{2,1},{3,2},{4,3},{5,4},{6,5},{7,6},{9,8},{10,9},{11,10},{12... | collective-permute-start | bytes 98312 | tf_op jit(solution)/shard_map/ppermute | solution.py:20
  158.8 2.4 %collective-permute-start.8 = (f32[1,64,128]{2,1,0:T(8,128)S(1)}, f32[1,64,128]{2,1,0:T(8,128)S(1)}, u32[]{:S(2)}, u32[]{:S(2)}) collective-permute-start(f32[1,64,128]{2,1,0:T(8,128)S(1)} %get-tuple-element.7), channel_id=1, source_target_pairs={{0,1},{1,2},{2,3},{3,4},{4,5},{5,6},{6,7},{8,9},{9,10},{10,11},{11... | collective-permute-start | bytes 98312 | tf_op jit(solution)/shard_map/ppermute | solution.py:18
  161.2 1.5 constant_dynamic-slice_fusion
  162.7 0.0 collective-permute-done.7
  162.7 2.2 %collective-permute-done.8 = f32[1,64,128]{2,1,0:T(8,128)S(1)} collective-permute-done((f32[1,64,128]{2,1,0:T(8,128)S(1)}, f32[1,64,128]{2,1,0:T(8,128)S(1)}, u32[]{:S(2)}, u32[]{:S(2)}) %collective-permute-start.8) | collective-permute-done | bytes 32800 | tf_op jit(solution)/shard_map/ppermute | solution.py:18
  164.9 1.2 select_maximum_fusion
  166.1 1.3 fusion.5
  167.5 0.7 fusion.12
  (14 shorter events, 0.5 us)
Async XLA Ops:
  7.2 70.9 %copy-start = (bf16[8192,32]{0,1:T(8,128)(2,1)S(1)}, bf16[8192,32]{0,1:T(8,128)(2,1)}, u32[]{:S(2)}) copy-start(bf16[8192,32]{0,1:T(8,128)(2,1)} %param.6) | copy-start | bytes 1572868
  7.2 148.9 %all-reduce.3.cloned.1.call-start = ((), (), s32[]{:S(2)}) async-start(), calls=%async_computation | async-start | bytes 524288 | tf_op jit(solution)/shard_map/psum | solution.py:65
  7.2 9.8 %collective-permute-start = (bf16[8192,32]{0,1:T(8,128)(2,1)}, bf16[8192,32]{0,1:T(8,128)(2,1)S(1)}, u32[]{:S(2)}, u32[]{:S(2)}) collective-permute-start(bf16[8192,32]{0,1:T(8,128)(2,1)} %param.6), channel_id=1, source_target_pairs={{0,1},{1,2},{2,3},{3,4},{4,5},{5,6},{6,7},{7,0},{8,9},{9,10},{10,1... | collective-permute-start | bytes 1572872 | tf_op jit(solution)/shard_map/ppermute | solution.py:48
  17.0 9.5 %collective-permute-start.1 = (bf16[8192,32]{0,1:T(8,128)(2,1)S(1)}, bf16[8192,32]{0,1:T(8,128)(2,1)S(1)}, u32[]{:S(2)}, u32[]{:S(2)}) collective-permute-start(bf16[8192,32]{0,1:T(8,128)(2,1)S(1)} %collective-permute-done), channel_id=1, source_target_pairs={{0,1},{1,2},{2,3},{3,4},{4,5},{5,6},{6,7},{7,0},{8,9},{9,10},{10,1... | collective-permute-start | bytes 1572872 | tf_op jit(solution)/shard_map/ppermute | solution.py:48
  26.5 9.5 %collective-permute-start.2 = (bf16[8192,32]{0,1:T(8,128)(2,1)S(1)}, bf16[8192,32]{0,1:T(8,128)(2,1)S(1)}, u32[]{:S(2)}, u32[]{:S(2)}) collective-permute-start(bf16[8192,32]{0,1:T(8,128)(2,1)S(1)} %collective-permute-done.1), channel_id=1, source_target_pairs={{0,1},{1,2},{2,3},{3,4},{4,5},{5,6},{6,7},{7,0},{8,9},{9,10},{10,1... | collective-permute-start | bytes 1572872 | tf_op jit(solution)/shard_map/ppermute | solution.py:48
  36.0 9.5 %collective-permute-start.3 = (bf16[8192,32]{0,1:T(8,128)(2,1)S(1)}, bf16[8192,32]{0,1:T(8,128)(2,1)S(1)}, u32[]{:S(2)}, u32[]{:S(2)}) collective-permute-start(bf16[8192,32]{0,1:T(8,128)(2,1)S(1)} %collective-permute-done.2), channel_id=1, source_target_pairs={{0,1},{1,2},{2,3},{3,4},{4,5},{5,6},{6,7},{7,0},{8,9},{9,10},{10,1... | collective-permute-start | bytes 1572872 | tf_op jit(solution)/shard_map/ppermute | solution.py:48
  45.5 9.5 %collective-permute-start.4 = (bf16[8192,32]{0,1:T(8,128)(2,1)S(1)}, bf16[8192,32]{0,1:T(8,128)(2,1)S(1)}, u32[]{:S(2)}, u32[]{:S(2)}) collective-permute-start(bf16[8192,32]{0,1:T(8,128)(2,1)S(1)} %collective-permute-done.3), channel_id=1, source_target_pairs={{0,1},{1,2},{2,3},{3,4},{4,5},{5,6},{6,7},{7,0},{8,9},{9,10},{10,1... | collective-permute-start | bytes 1572872 | tf_op jit(solution)/shard_map/ppermute | solution.py:48
  55.0 9.6 %collective-permute-start.5 = (bf16[8192,32]{0,1:T(8,128)(2,1)S(1)}, bf16[8192,32]{0,1:T(8,128)(2,1)}, u32[]{:S(2)}, u32[]{:S(2)}) collective-permute-start(bf16[8192,32]{0,1:T(8,128)(2,1)S(1)} %collective-permute-done.4), channel_id=1, source_target_pairs={{0,1},{1,2},{2,3},{3,4},{4,5},{5,6},{6,7},{7,0},{8,9},{9,10},{10,1... | collective-permute-start | bytes 1572872 | tf_op jit(solution)/shard_map/ppermute | solution.py:48
  64.6 9.7 %collective-permute-start.6 = (bf16[8192,32]{0,1:T(8,128)(2,1)}, bf16[8192,32]{0,1:T(8,128)(2,1)S(1)}, u32[]{:S(2)}, u32[]{:S(2)}) collective-permute-start(bf16[8192,32]{0,1:T(8,128)(2,1)} %collective-permute-done.5), channel_id=1, source_target_pairs={{0,1},{1,2},{2,3},{3,4},{4,5},{5,6},{6,7},{7,0},{8,9},{9,10},{10,1... | collective-permute-start | bytes 1572872 | tf_op jit(solution)/shard_map/ppermute | solution.py:48
  80.4 22.2 %copy-start.1 = (f32[32]{0:T(128)S(1)}, f32[32]{0:T(128)}, u32[]{:S(2)}) copy-start(f32[32]{0:T(128)} %param.7) | copy-start | bytes 388
  156.9 5.8 %collective-permute-start.7 = (f32[1,64,128]{2,1,0:T(8,128)S(1)}, f32[1,64,128]{2,1,0:T(8,128)S(1)}, u32[]{:S(2)}, u32[]{:S(2)}) collective-permute-start(f32[1,64,128]{2,1,0:T(8,128)S(1)} %get-tuple-element.6), channel_id=1, source_target_pairs={{1,0},{2,1},{3,2},{4,3},{5,4},{6,5},{7,6},{9,8},{10,9},{11,10},{12... | collective-permute-start | bytes 98312 | tf_op jit(solution)/shard_map/ppermute | solution.py:20
  158.8 6.1 %collective-permute-start.8 = (f32[1,64,128]{2,1,0:T(8,128)S(1)}, f32[1,64,128]{2,1,0:T(8,128)S(1)}, u32[]{:S(2)}, u32[]{:S(2)}) collective-permute-start(f32[1,64,128]{2,1,0:T(8,128)S(1)} %get-tuple-element.7), channel_id=1, source_target_pairs={{0,1},{1,2},{2,3},{3,4},{4,5},{5,6},{6,7},{8,9},{9,10},{10,11},{11... | collective-permute-start | bytes 98312 | tf_op jit(solution)/shard_map/ppermute | solution.py:18
Sparse Core Ops, SparseCore 0:
  120.2 35.8 all-reduce.2
